TPU v7x, 128 devices: a whole 4x4x4 slice. The times are simulated.
128 devices in a mesh: row: 8 (over z, core), col: 16 (over x, y).
Axes of the slice: x: 4, y: 4, z: 4, core: 2. Of those that a mesh axis runs over, the one named last changes fastest.
Arguments:
- block_values: bfloat16 [8, 16, 256, 128, 128], P('row', 'col'), may hold values from -1.2 to 1.2
- block_rows: int32 [8, 16, 256], P('row', 'col'), may hold values from 0 to 207, as said below
- block_cols: int32 [8, 16, 256], P('row', 'col'), may hold values from 0 to 103, as said below
- start_vectors: bfloat16 [212992, 256], P(('row', 'col')), may hold values from -6 to 6
- center: float32 [1], replicated, may hold values from -0.5 to -0.1
- half_width: float32 [1], replicated, may hold values from 0.9 to 1.3
- row_counts: int32 [128], replicated, may hold values from 7 to 19, as said below
Outputs:
- relaid: bfloat16 [311296, 256], P(('row', 'col'))
Inputs may be any that keep to these rules, and one draw needn't show every extreme that they name: `block_rows`: the first 13 entries of cell (r, c) are its diagonal blocks, at local row c * 13 + k; the rest are anywhere; positions may repeat, and repeated blocks add. `block_cols`: the first 13 entries of cell (r, c) are at local column r * 13 + k. `row_counts`: entries 2 i and 2 i + 1 sum to 26; entry 0 is larger than 13.
All inputs are finite; a program needn't handle non-finite values.
Results may differ from a plain program's by a relative error of at most 0.019.
Values may be sent and summed in bfloat16 or wider, within the bound.
A program may use at most 192 MiB of HBM per device.

v0:
```python
import math
import jax
import jax.numpy as jnp
from jax import lax
from jax.sharding import PartitionSpec as P


def swapped(block, axis, bit):
    count = lax.axis_size(axis)
    route = []
    for low in range(count):
        high = low | 1 << bit
        if high != low and high < count:
            route += [(low, high), (high, low)]
    return lax.ppermute(block, axis, route)


def block_images(values, row_ids, col_ids, panel_rows, out_blocks):
    orbitals = values.shape[-1]
    vec_count = panel_rows.shape[-1]
    blocks = panel_rows.reshape(-1, orbitals, vec_count)
    block_count = values.shape[0]
    group_size = math.gcd(block_count, 64)

    def add_group(row_images, group_items):
        group_values, group_rows, group_cols = group_items
        picked = blocks[group_cols]
        images = jnp.einsum(
            "gij,gjv->giv", group_values, picked, preferred_element_type=jnp.float32
        )
        return (row_images.at[group_rows].add(images), None)

    initial = jnp.zeros((out_blocks, orbitals, vec_count), jnp.float32)
    turns = block_count // group_size
    group_items = (
        values.reshape(turns, group_size, orbitals, orbitals),
        row_ids.reshape(turns, group_size),
        col_ids.reshape(turns, group_size),
    )
    row_images, _ = lax.scan(add_group, initial, group_items)
    return row_images.reshape(out_blocks * orbitals, vec_count)


def on_device(block_values, block_rows, block_cols, start_vectors, center, half_width, row_counts):
    orbitals = block_values.shape[-1]
    values = block_values.reshape(-1, orbitals, orbitals)
    row_ids = block_rows.reshape(-1)
    col_ids = block_cols.reshape(-1)
    own_rows, vec_count = start_vectors.shape
    own_blocks = own_rows // orbitals
    col_count = lax.axis_size("col")
    center_value = center[0]
    width_value = half_width[0]

    def image_of(vectors):
        panel_rows = lax.all_gather(vectors, "row", axis=0, tiled=True)
        cell_terms = block_images(values, row_ids, col_ids, panel_rows, col_count * own_blocks)
        return lax.psum_scatter(
            cell_terms.astype(jnp.bfloat16), "col", scatter_dimension=0, tiled=True
        ).astype(jnp.float32)

    source = start_vectors.astype(jnp.float32)
    first_image = image_of(start_vectors)
    first_step = ((first_image - center_value * source) / width_value).astype(jnp.bfloat16)
    second_image = image_of(first_step)
    second = (
        2.0 * (second_image - center_value * first_step.astype(jnp.float32)) / width_value - source
    ).astype(jnp.bfloat16)
    device = lax.axis_index("row") * col_count + lax.axis_index("col")
    parity = device % 2
    even_count = row_counts[device - parity]
    own_count = row_counts[device]
    start_block = parity * even_count
    half_blocks = own_blocks // 2
    capacity = own_blocks + half_blocks
    partner = swapped(second, ("row", "col"), 0)
    window = jnp.where(
        parity == 0, jnp.concatenate([second, partner], 0), jnp.concatenate([partner, second], 0)
    )
    window_low = parity * 0
    padded = jnp.concatenate([window, jnp.zeros((capacity * orbitals, vec_count), jnp.bfloat16)], 0)
    selected = lax.dynamic_slice_in_dim(padded, start_block * orbitals, capacity * orbitals, 0)
    live_rows = jnp.arange(capacity * orbitals, dtype=jnp.int32)[:, None] < own_count * orbitals
    return jnp.where(live_rows, selected, jnp.zeros_like(selected))


def solution(mesh):
    placed = (
        P("row", "col", None, None, None),
        P("row", "col", None),
        P("row", "col", None),
        P(("row", "col"), None),
        P(),
        P(),
        P(),
    )
    return jax.shard_map(
        on_device, mesh=mesh, in_specs=placed, out_specs=P(("row", "col"), None), check_vma=False
    )
```

profile of v0, /device:TPU:0, one launch (start us, length us, event | category | flops | bytes accessed | tf_op | source)
XLA Modules:
  0.0 645.1 jit_solution(17980662493797626057)
XLA Ops:
  6.5 0.0 all-gather.3.cloned.1.call-start
  6.5 0.7 all-gather.3.cloned.1.call-update
  7.3 0.0 reduce-scatter.3.cloned.1.call-start
  7.3 0.5 broadcast.113
  7.8 1.3 reduce.6
  9.1 0.1 reshape_reshape.12
  9.2 1.3 reduce.7
  10.5 0.1 reshape_reshape.14
  10.6 44.2 %all-gather.3.cloned.1.call-done = bf16[13312,256]{1,0:T(8,128)(2,1)} async-done(((bf16[1664,256]{1,0:T(8,128)(2,1)}), bf16[13312,256]{1,0:T(8,128)(2,1)}) %all-gather.3.cloned.1.call-update) | async-done | bytes 6815760 | tf_op jit(solution)/shard_map/all_gather | solution.py:56
  54.8 12.5 %broadcast.88.clone = f32[208,128,256]{2,1,0:T(8,128)} broadcast(f32[]{:T(128)} %constant.61.clone.1), dimensions={} | broadcast | bytes 27262980 | tf_op jit(solution)/shard_map/broadcast.15
  67.3 130.8 %while.20 = (s32[]{:T(128)}, f32[208,128,256]{2,1,0:T(8,128)}, s32[4,64]{1,0:T(4,128)S(1)}, bf16[4,64,128,128]{3,2,1,0:T(8,128)(2,1)}, s32[4,64]{1,0:T(4,128)S(1)}, /*index=5*/bf16[104,128,256]{2,1,0:T(8,128)(2,1)}, s32[]{:T(128)}) while((s32[]{:T(128)}, f32[208,128,256]{2,1,0:T(8,128)}, s32[4,64]{1,0:T(4,128)S(1)}, ...), condition=%wide.region_2.3_spmd, body=%wide.region_0.2_spmd.sunk | while | flops 538969472 | bytes 48240976 | solution.py:40
  67.3 5.7 gather_fusion
  73.0 7.3 %fusion.35 = f32[64,128,256]{2,1,0:T(8,128)} fusion(bf16[64,128,256]{2,1,0:T(8,128)(2,1)} %gather_fusion, bf16[4,64,128,128]{3,2,1,0:T(8,128)(2,1)} %get-tuple-element.200, s32[]{:T(128)} %get-tuple-element.190), kind=kOutput, calls=%fused_computation.4.clone.1 | convolution fusion | flops 536870912 | bytes 14680576 | tf_op jit(solution)/shard_map/while/body/eval_jaxpr/gij,gjv->giv/dot_general | solution.py:28
  80.3 19.6 %scatter_fusion = f32[208,128,256]{2,1,0:T(8,128)} fusion(f32[208,128,256]{2,1,0:T(8,128)} %get-tuple-element.191, s32[64]{0:T(128)S(1)} %get-tuple-element.173, f32[64,128,256]{2,1,0:T(8,128)} %fusion.35), kind=kCustom, calls=%fused_computation.2.clone.1 | custom fusion | flops 2097152 | bytes 25166080 | tf_op jit(solution)/shard_map/while/body/eval_jaxpr/scatter-add | solution.py:31
  99.9 5.7 gather_fusion
  105.6 7.3 %fusion.35 = f32[64,128,256]{2,1,0:T(8,128)} fusion(bf16[64,128,256]{2,1,0:T(8,128)(2,1)} %gather_fusion, bf16[4,64,128,128]{3,2,1,0:T(8,128)(2,1)} %get-tuple-element.200, s32[]{:T(128)} %get-tuple-element.190), kind=kOutput, calls=%fused_computation.4.clone.1 | convolution fusion | flops 536870912 | bytes 14680576 | tf_op jit(solution)/shard_map/while/body/eval_jaxpr/gij,gjv->giv/dot_general | solution.py:28
  112.9 19.7 %scatter_fusion = f32[208,128,256]{2,1,0:T(8,128)} fusion(f32[208,128,256]{2,1,0:T(8,128)} %get-tuple-element.191, s32[64]{0:T(128)S(1)} %get-tuple-element.173, f32[64,128,256]{2,1,0:T(8,128)} %fusion.35), kind=kCustom, calls=%fused_computation.2.clone.1 | custom fusion | flops 2097152 | bytes 25166080 | tf_op jit(solution)/shard_map/while/body/eval_jaxpr/scatter-add | solution.py:31
  132.7 5.7 gather_fusion
  138.4 7.3 %fusion.35 = f32[64,128,256]{2,1,0:T(8,128)} fusion(bf16[64,128,256]{2,1,0:T(8,128)(2,1)} %gather_fusion, bf16[4,64,128,128]{3,2,1,0:T(8,128)(2,1)} %get-tuple-element.200, s32[]{:T(128)} %get-tuple-element.190), kind=kOutput, calls=%fused_computation.4.clone.1 | convolution fusion | flops 536870912 | bytes 14680576 | tf_op jit(solution)/shard_map/while/body/eval_jaxpr/gij,gjv->giv/dot_general | solution.py:28
  145.7 19.8 %scatter_fusion = f32[208,128,256]{2,1,0:T(8,128)} fusion(f32[208,128,256]{2,1,0:T(8,128)} %get-tuple-element.191, s32[64]{0:T(128)S(1)} %get-tuple-element.173, f32[64,128,256]{2,1,0:T(8,128)} %fusion.35), kind=kCustom, calls=%fused_computation.2.clone.1 | custom fusion | flops 2097152 | bytes 25166080 | tf_op jit(solution)/shard_map/while/body/eval_jaxpr/scatter-add | solution.py:31
  165.5 5.7 gather_fusion
  171.2 7.3 %fusion.35 = f32[64,128,256]{2,1,0:T(8,128)} fusion(bf16[64,128,256]{2,1,0:T(8,128)(2,1)} %gather_fusion, bf16[4,64,128,128]{3,2,1,0:T(8,128)(2,1)} %get-tuple-element.200, s32[]{:T(128)} %get-tuple-element.190), kind=kOutput, calls=%fused_computation.4.clone.1 | convolution fusion | flops 536870912 | bytes 14680576 | tf_op jit(solution)/shard_map/while/body/eval_jaxpr/gij,gjv->giv/dot_general | solution.py:28
  178.5 19.6 %scatter_fusion = f32[208,128,256]{2,1,0:T(8,128)} fusion(f32[208,128,256]{2,1,0:T(8,128)} %get-tuple-element.191, s32[64]{0:T(128)S(1)} %get-tuple-element.173, f32[64,128,256]{2,1,0:T(8,128)} %fusion.35), kind=kCustom, calls=%fused_computation.2.clone.1 | custom fusion | flops 2097152 | bytes 25166080 | tf_op jit(solution)/shard_map/while/body/eval_jaxpr/scatter-add | solution.py:31
  198.1 15.5 %convert_element_type.30 = bf16[208,128,256]{2,1,0:T(8,128)(2,1)} convert(f32[208,128,256]{2,1,0:T(8,128)} %get-tuple-element.69) | non-fusion elementwise | flops 6815744 | bytes 40894464 | tf_op jit(solution)/shard_map/convert_element_type | solution.py:59
  213.6 0.0 copy-start
  213.6 0.0 reduce-scatter.3.cloned.1.call-update
  213.7 0.0 all-gather.5.cloned.1.call-start
  215.1 96.4 %reduce-scatter.3.cloned.1.call-done = bf16[1664,256]{1,0:T(8,128)(2,1)} async-done(((bf16[26624,256]{1,0:T(8,128)(2,1)}), bf16[1664,256]{1,0:T(8,128)(2,1)}) %reduce-scatter.3.cloned.1.call-update) | async-done | bytes 851984 | tf_op jit(solution)/shard_map/reduce_scatter | solution.py:58
  311.5 0.0 copy-done
  311.5 2.4 fusion.18
  313.9 0.0 all-gather.5.cloned.1.call-update
  313.9 0.0 reduce-scatter.5.cloned.1.call-start
  313.9 42.2 %all-gather.5.cloned.1.call-done = bf16[13312,256]{1,0:T(8,128)(2,1)} async-done(((bf16[1664,256]{1,0:T(8,128)(2,1)}), bf16[13312,256]{1,0:T(8,128)(2,1)}) %all-gather.5.cloned.1.call-update) | async-done | bytes 6815760 | tf_op jit(solution)/shard_map/all_gather | solution.py:56
  356.1 12.5 %broadcast.88 = f32[208,128,256]{2,1,0:T(8,128)} broadcast(f32[]{:T(128)} %constant.61.clone.1), dimensions={} | broadcast | bytes 27262980 | tf_op jit(solution)/shard_map/broadcast.15
  368.5 130.8 %while.21 = (s32[]{:T(128)}, f32[208,128,256]{2,1,0:T(8,128)}, s32[4,64]{1,0:T(4,128)S(1)}, bf16[4,64,128,128]{3,2,1,0:T(8,128)(2,1)}, s32[4,64]{1,0:T(4,128)S(1)}, /*index=5*/bf16[104,128,256]{2,1,0:T(8,128)(2,1)}, s32[]{:T(128)}) while((s32[]{:T(128)}, f32[208,128,256]{2,1,0:T(8,128)}, s32[4,64]{1,0:T(4,128)S(1)}, ...), condition=%wide.region_6.7_spmd, body=%wide.region_4.6_spmd.sunk | while | flops 538969472 | bytes 48240976 | solution.py:40
  368.6 5.7 gather_fusion.1
  374.3 7.3 %fusion.39 = f32[64,128,256]{2,1,0:T(8,128)} fusion(bf16[64,128,256]{2,1,0:T(8,128)(2,1)} %gather_fusion.1, bf16[4,64,128,128]{3,2,1,0:T(8,128)(2,1)} %get-tuple-element.221, s32[]{:T(128)} %get-tuple-element.211), kind=kOutput, calls=%fused_computation.17.clone.1 | convolution fusion | flops 536870912 | bytes 14680576 | tf_op jit(solution)/shard_map/while/body/eval_jaxpr/gij,gjv->giv/dot_general | solution.py:28
  381.6 19.6 %scatter_fusion.1 = f32[208,128,256]{2,1,0:T(8,128)} fusion(f32[208,128,256]{2,1,0:T(8,128)} %get-tuple-element.212, s32[64]{0:T(128)S(1)} %get-tuple-element.181, f32[64,128,256]{2,1,0:T(8,128)} %fusion.39), kind=kCustom, calls=%fused_computation.3.clone.1 | custom fusion | flops 2097152 | bytes 25166080 | tf_op jit(solution)/shard_map/while/body/eval_jaxpr/scatter-add | solution.py:31
  401.2 5.7 gather_fusion.1
  406.9 7.3 %fusion.39 = f32[64,128,256]{2,1,0:T(8,128)} fusion(bf16[64,128,256]{2,1,0:T(8,128)(2,1)} %gather_fusion.1, bf16[4,64,128,128]{3,2,1,0:T(8,128)(2,1)} %get-tuple-element.221, s32[]{:T(128)} %get-tuple-element.211), kind=kOutput, calls=%fused_computation.17.clone.1 | convolution fusion | flops 536870912 | bytes 14680576 | tf_op jit(solution)/shard_map/while/body/eval_jaxpr/gij,gjv->giv/dot_general | solution.py:28
  414.2 19.7 %scatter_fusion.1 = f32[208,128,256]{2,1,0:T(8,128)} fusion(f32[208,128,256]{2,1,0:T(8,128)} %get-tuple-element.212, s32[64]{0:T(128)S(1)} %get-tuple-element.181, f32[64,128,256]{2,1,0:T(8,128)} %fusion.39), kind=kCustom, calls=%fused_computation.3.clone.1 | custom fusion | flops 2097152 | bytes 25166080 | tf_op jit(solution)/shard_map/while/body/eval_jaxpr/scatter-add | solution.py:31
  434.0 5.7 gather_fusion.1
  439.7 7.3 %fusion.39 = f32[64,128,256]{2,1,0:T(8,128)} fusion(bf16[64,128,256]{2,1,0:T(8,128)(2,1)} %gather_fusion.1, bf16[4,64,128,128]{3,2,1,0:T(8,128)(2,1)} %get-tuple-element.221, s32[]{:T(128)} %get-tuple-element.211), kind=kOutput, calls=%fused_computation.17.clone.1 | convolution fusion | flops 536870912 | bytes 14680576 | tf_op jit(solution)/shard_map/while/body/eval_jaxpr/gij,gjv->giv/dot_general | solution.py:28
  447.0 19.8 %scatter_fusion.1 = f32[208,128,256]{2,1,0:T(8,128)} fusion(f32[208,128,256]{2,1,0:T(8,128)} %get-tuple-element.212, s32[64]{0:T(128)S(1)} %get-tuple-element.181, f32[64,128,256]{2,1,0:T(8,128)} %fusion.39), kind=kCustom, calls=%fused_computation.3.clone.1 | custom fusion | flops 2097152 | bytes 25166080 | tf_op jit(solution)/shard_map/while/body/eval_jaxpr/scatter-add | solution.py:31
  466.8 5.7 gather_fusion.1
  472.5 7.3 %fusion.39 = f32[64,128,256]{2,1,0:T(8,128)} fusion(bf16[64,128,256]{2,1,0:T(8,128)(2,1)} %gather_fusion.1, bf16[4,64,128,128]{3,2,1,0:T(8,128)(2,1)} %get-tuple-element.221, s32[]{:T(128)} %get-tuple-element.211), kind=kOutput, calls=%fused_computation.17.clone.1 | convolution fusion | flops 536870912 | bytes 14680576 | tf_op jit(solution)/shard_map/while/body/eval_jaxpr/gij,gjv->giv/dot_general | solution.py:28
  479.8 19.6 %scatter_fusion.1 = f32[208,128,256]{2,1,0:T(8,128)} fusion(f32[208,128,256]{2,1,0:T(8,128)} %get-tuple-element.212, s32[64]{0:T(128)S(1)} %get-tuple-element.181, f32[64,128,256]{2,1,0:T(8,128)} %fusion.39), kind=kCustom, calls=%fused_computation.3.clone.1 | custom fusion | flops 2097152 | bytes 25166080 | tf_op jit(solution)/shard_map/while/body/eval_jaxpr/scatter-add | solution.py:31
  499.4 15.5 %convert_element_type.35 = bf16[208,128,256]{2,1,0:T(8,128)(2,1)} convert(f32[208,128,256]{2,1,0:T(8,128)} %get-tuple-element.70) | non-fusion elementwise | flops 6815744 | bytes 40894464 | tf_op jit(solution)/shard_map/convert_element_type | solution.py:59
  514.9 0.0 copy-start.1
  514.9 0.0 copy-start.2
  514.9 0.0 reduce-scatter.5.cloned.1.call-update
  514.9 97.9 %reduce-scatter.5.cloned.1.call-done = bf16[1664,256]{1,0:T(8,128)(2,1)} async-done(((bf16[26624,256]{1,0:T(8,128)(2,1)}), bf16[1664,256]{1,0:T(8,128)(2,1)}) %reduce-scatter.5.cloned.1.call-update) | async-done | bytes 851984 | tf_op jit(solution)/shard_map/reduce_scatter | solution.py:58
  612.8 0.0 copy-done.1
  612.8 1.9 fusion.19
  614.7 0.9 collective-permute-start
  615.6 0.0 copy-done.2
  615.6 0.6 fusion.21
  617.5 17.6 %collective-permute-done = bf16[1664,256]{1,0:T(8,128)(2,1)S(1)} collective-permute-done((bf16[1664,256]{1,0:T(8,128)(2,1)S(1)}, bf16[1664,256]{1,0:T(8,128)(2,1)S(1)}, u32[]{:S(2)}, u32[]{:S(2)}) %collective-permute-start) | collective-permute-done | bytes 852000 | tf_op jit(solution)/shard_map/ppermute | solution.py:15
  635.1 0.4 maximum_select_fusion
  635.5 3.1 fusion.20
  (17 shorter events, 0.1 us)
Async XLA Ops:
  6.5 48.3 %all-gather.3.cloned.1.call-start = ((), (), s32[]{:S(2)}) async-start(), calls=%async_computation.2 | async-start | bytes 7667712 | tf_op jit(solution)/shard_map/all_gather | solution.py:56
  7.3 304.2 %reduce-scatter.3.cloned.1.call-start = ((), (), s32[]{:S(2)}) async-start(), calls=%async_computation.3 | async-start | bytes 14483456 | tf_op jit(solution)/shard_map/reduce_scatter | solution.py:58
  213.6 97.9 %copy-start = (bf16[1664,256]{1,0:T(8,128)(2,1)S(1)}, bf16[1664,256]{1,0:T(8,128)(2,1)}, u32[]{:S(2)}) copy-start(bf16[1664,256]{1,0:T(8,128)(2,1)} %param.14) | copy-start | bytes 2555908
  213.7 142.4 %all-gather.5.cloned.1.call-start = ((), (), s32[]{:S(2)}) async-start(), calls=%async_computation.4 | async-start | bytes 7667712 | tf_op jit(solution)/shard_map/all_gather | solution.py:56
  313.9 298.9 %reduce-scatter.5.cloned.1.call-start = ((), (), s32[]{:S(2)}) async-start(), calls=%async_computation.5 | async-start | bytes 14483456 | tf_op jit(solution)/shard_map/reduce_scatter | solution.py:58
  514.9 97.9 %copy-start.1 = (bf16[1664,256]{1,0:T(8,128)(2,1)S(1)}, bf16[1664,256]{1,0:T(8,128)(2,1)}, u32[]{:S(2)}) copy-start(bf16[1664,256]{1,0:T(8,128)(2,1)} %reduce-scatter.3.cloned.1.call-done) | copy-start | bytes 2555908
  514.9 100.7 %copy-start.2 = (s32[128]{0:T(128)S(1)}, s32[128]{0:T(128)}, u32[]{:S(2)}) copy-start(s32[128]{0:T(128)} %param.17) | copy-start | bytes 1540
  614.7 20.4 %collective-permute-start = (bf16[1664,256]{1,0:T(8,128)(2,1)S(1)}, bf16[1664,256]{1,0:T(8,128)(2,1)S(1)}, u32[]{:S(2)}, u32[]{:S(2)}) collective-permute-start(bf16[1664,256]{1,0:T(8,128)(2,1)S(1)} %fusion.19), channel_id=1, source_target_pairs={{0,1},{1,0},{2,3},{3,2},{4,5},{5,4},{6,7},{7,6},{8,9},{9,8},{10,11... | collective-permute-start | bytes 2555912 | tf_op jit(solution)/shard_map/ppermute | solution.py:15
Sparse Core Ops, SparseCore 0:
  9.0 45.7 all-gather.2
  213.8 97.6 reduce-scatter.2
  314.0 42.0 all-gather.4
  515.1 97.6 reduce-scatter.4
where the time goes:
time: 646 us; the launch traced here: 645 us
  waiting for transfers between devices  299 us (46%)
  other arithmetic  199 us (31%)
  local copies, waits for them, and re-layouts  71.9 us (11%)
  matrix products  58.4 us (9%)
  between operations  15.8 us (2%)
    reduce_scatter x2, waiting for transfers between devices, image_of(): lax.psum_scatter(cell_terms.astype(jnp.bfloat16), 'col', scatter_dimensio...  194 us
    scatter-add x8, other arithmetic, add_group(): return (row_images.at[group_rows].add(images), None)  157 us
    all_gather x2, waiting for transfers between devices, image_of(): panel_rows = lax.all_gather(vectors, 'row', axis=0, tiled=True)  86.3 us
    dot_general x8, matrix products, add_group(): jnp.einsum('gij,gjv->giv', group_values, picked, preferred_element_type=j...  58.4 us
    gather x8, local copies, waits for them, and re-layouts, add_group(): picked = blocks[group_cols]  45.7 us
    convert_element_type x2, other arithmetic, image_of(): cell_terms.astype(jnp.bfloat16)  31.1 us
    another operation x2, local copies, waits for them, and re-layouts  24.9 us
    ppermute x1, waiting for transfers between devices, swapped(): return lax.ppermute(block, axis, route)  17.6 us
  transfers between devices with their start and end apart: 5, of which 5 were waited for; matrix products, arithmetic and copies ran while one was open for 1% of the time, Pallas kernels for 0%

commit v1 on v0

--- a/solution.py
+++ b/solution.py
@@ -53,7 +53,8 @@
     width_value = half_width[0]
 
     def image_of(vectors):
-        panel_rows = lax.all_gather(vectors, "row", axis=0, tiled=True)
+        outgoing = jnp.stack([vectors] * lax.axis_size("row"))
+        panel_rows = jnp.concatenate(lax.all_to_all(outgoing, "row", 0, 0), axis=0)
         cell_terms = block_images(values, row_ids, col_ids, panel_rows, col_count * own_blocks)
         return lax.psum_scatter(
             cell_terms.astype(jnp.bfloat16), "col", scatter_dimension=0, tiled=True

time: 646 us -> 726 us (1.12)
  waiting for transfers between devices: 299 us -> 363 us
  starting transfers between devices: 1 us -> 11.5 us
  local copies, waits for them, and re-layouts: 71.9 us -> 79.5 us
    all_to_all x0 -> x2, waiting for transfers between devices: none -> 153 us  [image_of(): panel_rows = jnp.concatenate(lax.all_to_all(outgoing, 'row', 0, 0), axis=0)]
    all_gather x2 -> x0, waiting for transfers between devices: 86.3 us -> none  [image_of(): panel_rows = lax.all_gather(vectors, 'row', axis=0, tiled=True)]
    all_to_all x0 -> x2, starting transfers between devices: none -> 10.4 us  [image_of(): panel_rows = jnp.concatenate(lax.all_to_all(outgoing, 'row', 0, 0), axis=0)]
    another operation x2 -> x4, local copies, waits for them, and re-layouts: 24.9 us -> 32.5 us
  transfers between devices with their start and end apart: 5 -> 5, of which waited for: 5 -> 5; matrix products, arithmetic and copies ran while one was open for 1% -> 0% of each run, Pallas kernels for 0% -> 0%
where the time goes in v1:
time: 726 us; the launch traced here: 725 us
  waiting for transfers between devices  363 us (50%)
  other arithmetic  197 us (27%)
  local copies, waits for them, and re-layouts  79.5 us (11%)
  matrix products  58.4 us (8%)
  between operations  16.1 us (2%)
  starting transfers between devices  11.5 us (2%)
    reduce_scatter x2, waiting for transfers between devices, image_of(): lax.psum_scatter(cell_terms.astype(jnp.bfloat16), 'col', scatter_dimensio...  192 us
    scatter-add x8, other arithmetic, add_group(): return (row_images.at[group_rows].add(images), None)  157 us
    all_to_all x2, waiting for transfers between devices, image_of(): panel_rows = jnp.concatenate(lax.all_to_all(outgoing, 'row', 0, 0), axis=0)  153 us
    dot_general x8, matrix products, add_group(): jnp.einsum('gij,gjv->giv', group_values, picked, preferred_element_type=j...  58.4 us
    gather x8, local copies, waits for them, and re-layouts, add_group(): picked = blocks[group_cols]  45.7 us
    convert_element_type x2, other arithmetic, image_of(): cell_terms.astype(jnp.bfloat16)  31.1 us
    another operation x2, local copies, waits for them, and re-layouts  24.9 us
    ppermute x1, waiting for transfers between devices, swapped(): return lax.ppermute(block, axis, route)  17.6 us
  transfers between devices with their start and end apart: 5, of which 5 were waited for; matrix products, arithmetic and copies ran while one was open for 0% of the time, Pallas kernels for 0%

profile of v1, /device:TPU:0, one launch (start us, length us, event | category | flops | bytes accessed | tf_op | source)
XLA Modules:
  0.0 724.8 jit_solution(6373839568551871150)
XLA Ops:
  6.5 4.4 stack.4
  10.9 0.0 copy-start.3
  10.9 0.0 copy-start.4
  10.9 5.6 all-to-all-start
  16.5 0.0 reduce-scatter.3.cloned.1.call-start
  16.5 0.5 broadcast.117
  17.0 0.0 copy-done.3
  17.0 0.6 reduce.6
  17.6 0.1 reshape_reshape.18
  17.7 0.0 copy-done.4
  17.7 0.6 reduce.7
  18.3 0.1 reshape_reshape.20
  18.4 76.0 %all-to-all-done = bf16[8,1664,256]{2,1,0:T(8,128)(2,1)} async-done(((bf16[8,1664,256]{2,1,0:T(8,128)(2,1)}), bf16[8,1664,256]{2,1,0:T(8,128)(2,1)}, u32[]{:S(2)}, u32[]{:S(2)}) %all-to-all-start) | async-done | bytes 6815776 | tf_op jit(solution)/shard_map/all_to_all | solution.py:57
  94.3 12.5 %broadcast.92.clone = f32[208,128,256]{2,1,0:T(8,128)} broadcast(f32[]{:T(128)} %constant.61.clone.1), dimensions={} | broadcast | bytes 27262980 | tf_op jit(solution)/shard_map/broadcast.15
  106.8 130.8 %while.20 = (s32[]{:T(128)}, f32[208,128,256]{2,1,0:T(8,128)}, s32[4,64]{1,0:T(4,128)S(1)}, bf16[4,64,128,128]{3,2,1,0:T(8,128)(2,1)}, s32[4,64]{1,0:T(4,128)S(1)}, /*index=5*/bf16[104,128,256]{2,1,0:T(8,128)(2,1)}, s32[]{:T(128)}) while((s32[]{:T(128)}, f32[208,128,256]{2,1,0:T(8,128)}, s32[4,64]{1,0:T(4,128)S(1)}, ...), condition=%wide.region_2.3_spmd, body=%wide.region_0.2_spmd.sunk | while | flops 538969472 | bytes 48240976 | solution.py:40
  106.8 5.7 gather_fusion
  112.5 7.3 %fusion.35 = f32[64,128,256]{2,1,0:T(8,128)} fusion(bf16[64,128,256]{2,1,0:T(8,128)(2,1)} %gather_fusion, bf16[4,64,128,128]{3,2,1,0:T(8,128)(2,1)} %get-tuple-element.200, s32[]{:T(128)} %get-tuple-element.190), kind=kOutput, calls=%fused_computation.4.clone.1 | convolution fusion | flops 536870912 | bytes 14680576 | tf_op jit(solution)/shard_map/while/body/eval_jaxpr/gij,gjv->giv/dot_general | solution.py:28
  119.8 19.6 %scatter_fusion = f32[208,128,256]{2,1,0:T(8,128)} fusion(f32[208,128,256]{2,1,0:T(8,128)} %get-tuple-element.191, s32[64]{0:T(128)S(1)} %get-tuple-element.173, f32[64,128,256]{2,1,0:T(8,128)} %fusion.35), kind=kCustom, calls=%fused_computation.2.clone.1 | custom fusion | flops 2097152 | bytes 25166080 | tf_op jit(solution)/shard_map/while/body/eval_jaxpr/scatter-add | solution.py:31
  139.4 5.7 gather_fusion
  145.1 7.3 %fusion.35 = f32[64,128,256]{2,1,0:T(8,128)} fusion(bf16[64,128,256]{2,1,0:T(8,128)(2,1)} %gather_fusion, bf16[4,64,128,128]{3,2,1,0:T(8,128)(2,1)} %get-tuple-element.200, s32[]{:T(128)} %get-tuple-element.190), kind=kOutput, calls=%fused_computation.4.clone.1 | convolution fusion | flops 536870912 | bytes 14680576 | tf_op jit(solution)/shard_map/while/body/eval_jaxpr/gij,gjv->giv/dot_general | solution.py:28
  152.4 19.7 %scatter_fusion = f32[208,128,256]{2,1,0:T(8,128)} fusion(f32[208,128,256]{2,1,0:T(8,128)} %get-tuple-element.191, s32[64]{0:T(128)S(1)} %get-tuple-element.173, f32[64,128,256]{2,1,0:T(8,128)} %fusion.35), kind=kCustom, calls=%fused_computation.2.clone.1 | custom fusion | flops 2097152 | bytes 25166080 | tf_op jit(solution)/shard_map/while/body/eval_jaxpr/scatter-add | solution.py:31
  172.2 5.7 gather_fusion
  177.9 7.3 %fusion.35 = f32[64,128,256]{2,1,0:T(8,128)} fusion(bf16[64,128,256]{2,1,0:T(8,128)(2,1)} %gather_fusion, bf16[4,64,128,128]{3,2,1,0:T(8,128)(2,1)} %get-tuple-element.200, s32[]{:T(128)} %get-tuple-element.190), kind=kOutput, calls=%fused_computation.4.clone.1 | convolution fusion | flops 536870912 | bytes 14680576 | tf_op jit(solution)/shard_map/while/body/eval_jaxpr/gij,gjv->giv/dot_general | solution.py:28
  185.2 19.8 %scatter_fusion = f32[208,128,256]{2,1,0:T(8,128)} fusion(f32[208,128,256]{2,1,0:T(8,128)} %get-tuple-element.191, s32[64]{0:T(128)S(1)} %get-tuple-element.173, f32[64,128,256]{2,1,0:T(8,128)} %fusion.35), kind=kCustom, calls=%fused_computation.2.clone.1 | custom fusion | flops 2097152 | bytes 25166080 | tf_op jit(solution)/shard_map/while/body/eval_jaxpr/scatter-add | solution.py:31
  205.0 5.7 gather_fusion
  210.7 7.3 %fusion.35 = f32[64,128,256]{2,1,0:T(8,128)} fusion(bf16[64,128,256]{2,1,0:T(8,128)(2,1)} %gather_fusion, bf16[4,64,128,128]{3,2,1,0:T(8,128)(2,1)} %get-tuple-element.200, s32[]{:T(128)} %get-tuple-element.190), kind=kOutput, calls=%fused_computation.4.clone.1 | convolution fusion | flops 536870912 | bytes 14680576 | tf_op jit(solution)/shard_map/while/body/eval_jaxpr/gij,gjv->giv/dot_general | solution.py:28
  218.0 19.6 %scatter_fusion = f32[208,128,256]{2,1,0:T(8,128)} fusion(f32[208,128,256]{2,1,0:T(8,128)} %get-tuple-element.191, s32[64]{0:T(128)S(1)} %get-tuple-element.173, f32[64,128,256]{2,1,0:T(8,128)} %fusion.35), kind=kCustom, calls=%fused_computation.2.clone.1 | custom fusion | flops 2097152 | bytes 25166080 | tf_op jit(solution)/shard_map/while/body/eval_jaxpr/scatter-add | solution.py:31
  237.6 15.5 %convert_element_type.30 = bf16[208,128,256]{2,1,0:T(8,128)(2,1)} convert(f32[208,128,256]{2,1,0:T(8,128)} %get-tuple-element.69) | non-fusion elementwise | flops 6815744 | bytes 40894464 | tf_op jit(solution)/shard_map/convert_element_type | solution.py:60
  253.1 0.0 copy-start
  253.1 0.0 reduce-scatter.3.cloned.1.call-update
  254.5 96.4 %reduce-scatter.3.cloned.1.call-done = bf16[1664,256]{1,0:T(8,128)(2,1)} async-done(((bf16[26624,256]{1,0:T(8,128)(2,1)}), bf16[1664,256]{1,0:T(8,128)(2,1)}) %reduce-scatter.3.cloned.1.call-update) | async-done | bytes 851984 | tf_op jit(solution)/shard_map/reduce_scatter | solution.py:59
  350.9 0.0 copy-done
  350.9 1.5 fusion.18
  352.4 3.2 stack.5
  355.6 4.8 all-to-all-start.1
  360.4 0.2 reduce-scatter.5.cloned.1.call-start
  360.7 77.5 %all-to-all-done.1 = bf16[8,1664,256]{2,1,0:T(8,128)(2,1)} async-done(((bf16[8,1664,256]{2,1,0:T(8,128)(2,1)}), bf16[8,1664,256]{2,1,0:T(8,128)(2,1)}, u32[]{:S(2)}, u32[]{:S(2)}) %all-to-all-start.1) | async-done | bytes 6815776 | tf_op jit(solution)/shard_map/all_to_all | solution.py:57
  438.2 12.5 %broadcast.92 = f32[208,128,256]{2,1,0:T(8,128)} broadcast(f32[]{:T(128)} %constant.61.clone.1), dimensions={} | broadcast | bytes 27262980 | tf_op jit(solution)/shard_map/broadcast.15
  450.6 130.8 %while.21 = (s32[]{:T(128)}, f32[208,128,256]{2,1,0:T(8,128)}, s32[4,64]{1,0:T(4,128)S(1)}, bf16[4,64,128,128]{3,2,1,0:T(8,128)(2,1)}, s32[4,64]{1,0:T(4,128)S(1)}, /*index=5*/bf16[104,128,256]{2,1,0:T(8,128)(2,1)}, s32[]{:T(128)}) while((s32[]{:T(128)}, f32[208,128,256]{2,1,0:T(8,128)}, s32[4,64]{1,0:T(4,128)S(1)}, ...), condition=%wide.region_6.7_spmd, body=%wide.region_4.6_spmd.sunk | while | flops 538969472 | bytes 48240976 | solution.py:40
  450.6 5.7 gather_fusion.1
  456.3 7.3 %fusion.39 = f32[64,128,256]{2,1,0:T(8,128)} fusion(bf16[64,128,256]{2,1,0:T(8,128)(2,1)} %gather_fusion.1, bf16[4,64,128,128]{3,2,1,0:T(8,128)(2,1)} %get-tuple-element.221, s32[]{:T(128)} %get-tuple-element.211), kind=kOutput, calls=%fused_computation.17.clone.1 | convolution fusion | flops 536870912 | bytes 14680576 | tf_op jit(solution)/shard_map/while/body/eval_jaxpr/gij,gjv->giv/dot_general | solution.py:28
  463.6 19.6 %scatter_fusion.1 = f32[208,128,256]{2,1,0:T(8,128)} fusion(f32[208,128,256]{2,1,0:T(8,128)} %get-tuple-element.212, s32[64]{0:T(128)S(1)} %get-tuple-element.181, f32[64,128,256]{2,1,0:T(8,128)} %fusion.39), kind=kCustom, calls=%fused_computation.3.clone.1 | custom fusion | flops 2097152 | bytes 25166080 | tf_op jit(solution)/shard_map/while/body/eval_jaxpr/scatter-add | solution.py:31
  483.3 5.7 gather_fusion.1
  489.0 7.3 %fusion.39 = f32[64,128,256]{2,1,0:T(8,128)} fusion(bf16[64,128,256]{2,1,0:T(8,128)(2,1)} %gather_fusion.1, bf16[4,64,128,128]{3,2,1,0:T(8,128)(2,1)} %get-tuple-element.221, s32[]{:T(128)} %get-tuple-element.211), kind=kOutput, calls=%fused_computation.17.clone.1 | convolution fusion | flops 536870912 | bytes 14680576 | tf_op jit(solution)/shard_map/while/body/eval_jaxpr/gij,gjv->giv/dot_general | solution.py:28
  496.3 19.7 %scatter_fusion.1 = f32[208,128,256]{2,1,0:T(8,128)} fusion(f32[208,128,256]{2,1,0:T(8,128)} %get-tuple-element.212, s32[64]{0:T(128)S(1)} %get-tuple-element.181, f32[64,128,256]{2,1,0:T(8,128)} %fusion.39), kind=kCustom, calls=%fused_computation.3.clone.1 | custom fusion | flops 2097152 | bytes 25166080 | tf_op jit(solution)/shard_map/while/body/eval_jaxpr/scatter-add | solution.py:31
  516.0 5.7 gather_fusion.1
  521.7 7.3 %fusion.39 = f32[64,128,256]{2,1,0:T(8,128)} fusion(bf16[64,128,256]{2,1,0:T(8,128)(2,1)} %gather_fusion.1, bf16[4,64,128,128]{3,2,1,0:T(8,128)(2,1)} %get-tuple-element.221, s32[]{:T(128)} %get-tuple-element.211), kind=kOutput, calls=%fused_computation.17.clone.1 | convolution fusion | flops 536870912 | bytes 14680576 | tf_op jit(solution)/shard_map/while/body/eval_jaxpr/gij,gjv->giv/dot_general | solution.py:28
  529.0 19.8 %scatter_fusion.1 = f32[208,128,256]{2,1,0:T(8,128)} fusion(f32[208,128,256]{2,1,0:T(8,128)} %get-tuple-element.212, s32[64]{0:T(128)S(1)} %get-tuple-element.181, f32[64,128,256]{2,1,0:T(8,128)} %fusion.39), kind=kCustom, calls=%fused_computation.3.clone.1 | custom fusion | flops 2097152 | bytes 25166080 | tf_op jit(solution)/shard_map/while/body/eval_jaxpr/scatter-add | solution.py:31
  548.8 5.7 gather_fusion.1
  554.6 7.3 %fusion.39 = f32[64,128,256]{2,1,0:T(8,128)} fusion(bf16[64,128,256]{2,1,0:T(8,128)(2,1)} %gather_fusion.1, bf16[4,64,128,128]{3,2,1,0:T(8,128)(2,1)} %get-tuple-element.221, s32[]{:T(128)} %get-tuple-element.211), kind=kOutput, calls=%fused_computation.17.clone.1 | convolution fusion | flops 536870912 | bytes 14680576 | tf_op jit(solution)/shard_map/while/body/eval_jaxpr/gij,gjv->giv/dot_general | solution.py:28
  561.9 19.6 %scatter_fusion.1 = f32[208,128,256]{2,1,0:T(8,128)} fusion(f32[208,128,256]{2,1,0:T(8,128)} %get-tuple-element.212, s32[64]{0:T(128)S(1)} %get-tuple-element.181, f32[64,128,256]{2,1,0:T(8,128)} %fusion.39), kind=kCustom, calls=%fused_computation.3.clone.1 | custom fusion | flops 2097152 | bytes 25166080 | tf_op jit(solution)/shard_map/while/body/eval_jaxpr/scatter-add | solution.py:31
  581.5 15.5 %convert_element_type.35 = bf16[208,128,256]{2,1,0:T(8,128)(2,1)} convert(f32[208,128,256]{2,1,0:T(8,128)} %get-tuple-element.70) | non-fusion elementwise | flops 6815744 | bytes 40894464 | tf_op jit(solution)/shard_map/convert_element_type | solution.py:60
  597.0 0.0 copy-start.1
  597.0 0.0 copy-start.2
  597.0 0.0 reduce-scatter.5.cloned.1.call-update
  597.0 95.2 %reduce-scatter.5.cloned.1.call-done = bf16[1664,256]{1,0:T(8,128)(2,1)} async-done(((bf16[26624,256]{1,0:T(8,128)(2,1)}), bf16[1664,256]{1,0:T(8,128)(2,1)}) %reduce-scatter.5.cloned.1.call-update) | async-done | bytes 851984 | tf_op jit(solution)/shard_map/reduce_scatter | solution.py:59
  692.2 0.0 copy-done.1
  692.2 1.9 fusion.19
  694.1 0.9 collective-permute-start
  694.9 0.0 copy-done.2
  694.9 0.6 fusion.21
  696.8 17.6 %collective-permute-done = bf16[1664,256]{1,0:T(8,128)(2,1)S(1)} collective-permute-done((bf16[1664,256]{1,0:T(8,128)(2,1)S(1)}, bf16[1664,256]{1,0:T(8,128)(2,1)S(1)}, u32[]{:S(2)}, u32[]{:S(2)}) %collective-permute-start) | collective-permute-done | bytes 852000 | tf_op jit(solution)/shard_map/ppermute | solution.py:15
  714.5 0.4 maximum_select_fusion
  714.8 3.1 fusion.20
  (17 shorter events, 0.1 us)
Async XLA Ops:
  10.9 6.1 copy-start.3
  10.9 6.8 copy-start.4
  10.9 83.4 %all-to-all-start = ((bf16[8,1664,256]{2,1,0:T(8,128)(2,1)}), bf16[8,1664,256]{2,1,0:T(8,128)(2,1)}, u32[]{:S(2)}, u32[]{:S(2)}) async-start(bf16[8,1664,256]{2,1,0:T(8,128)(2,1)} %stack.4), calls=%async_computation | async-start | bytes 13631488 | tf_op jit(solution)/shard_map/all_to_all | solution.py:57
  16.5 334.5 %reduce-scatter.3.cloned.1.call-start = ((), (), s32[]{:S(2)}) async-start(), calls=%async_computation.4 | async-start | bytes 14483456 | tf_op jit(solution)/shard_map/reduce_scatter | solution.py:59
  253.1 97.8 %copy-start = (bf16[1664,256]{1,0:T(8,128)(2,1)S(1)}, bf16[1664,256]{1,0:T(8,128)(2,1)}, u32[]{:S(2)}) copy-start(bf16[1664,256]{1,0:T(8,128)(2,1)} %param.14) | copy-start | bytes 2555908
  355.6 82.5 %all-to-all-start.1 = ((bf16[8,1664,256]{2,1,0:T(8,128)(2,1)}), bf16[8,1664,256]{2,1,0:T(8,128)(2,1)}, u32[]{:S(2)}, u32[]{:S(2)}) async-start(bf16[8,1664,256]{2,1,0:T(8,128)(2,1)} %stack.5), calls=%async_computation.2 | async-start | bytes 13631488 | tf_op jit(solution)/shard_map/all_to_all | solution.py:57
  360.4 331.7 %reduce-scatter.5.cloned.1.call-start = ((), (), s32[]{:S(2)}) async-start(), calls=%async_computation.5 | async-start | bytes 14483456 | tf_op jit(solution)/shard_map/reduce_scatter | solution.py:59
  597.0 95.2 %copy-start.1 = (bf16[1664,256]{1,0:T(8,128)(2,1)S(1)}, bf16[1664,256]{1,0:T(8,128)(2,1)}, u32[]{:S(2)}) copy-start(bf16[1664,256]{1,0:T(8,128)(2,1)} %reduce-scatter.3.cloned.1.call-done) | copy-start | bytes 2555908
  597.0 98.0 %copy-start.2 = (s32[128]{0:T(128)S(1)}, s32[128]{0:T(128)}, u32[]{:S(2)}) copy-start(s32[128]{0:T(128)} %param.17) | copy-start | bytes 1540
  694.1 20.4 %collective-permute-start = (bf16[1664,256]{1,0:T(8,128)(2,1)S(1)}, bf16[1664,256]{1,0:T(8,128)(2,1)S(1)}, u32[]{:S(2)}, u32[]{:S(2)}) collective-permute-start(bf16[1664,256]{1,0:T(8,128)(2,1)S(1)} %fusion.19), channel_id=1, source_target_pairs={{0,1},{1,0},{2,3},{3,2},{4,5},{5,4},{6,7},{7,6},{8,9},{9,8},{10,11... | collective-permute-start | bytes 2555912 | tf_op jit(solution)/shard_map/ppermute | solution.py:15
Sparse Core Ops, SparseCore 0:
  253.3 97.5 reduce-scatter.2
  597.1 94.9 reduce-scatter.4
